TPU v7x, 32 devices: a whole 2x2x4 slice. The times are simulated.
32 devices in a mesh: sub: 8 (over y, x, core), coarse: 4 (over z).
Axes of the slice: x: 2, y: 2, z: 4, core: 2. Of those that a mesh axis runs over, the one named last changes fastest.
Arguments:
- right_side: float32 [8, 4, 128, 128], P('sub', 'coarse'), may hold values from -150 to 150
- diagonal: float32 [8, 4, 128, 128], P('sub', 'coarse'), may hold values from 2 to 8
- cell_link: float32 [8, 4, 128, 128], P('sub', 'coarse'), may hold values from 0.2 to 0.9
- block_inverse: float32 [8, 4, 128, 128, 128], P('sub', 'coarse'), may hold values from -1 to 1
- coupling: float32 [8, 4, 4, 128, 128], P('sub', 'coarse'), may hold values from -0.26516503 to 0.26516503
- coarse_basis: float32 [8, 4, 128, 128], P('sub', 'coarse'), may hold values from -6 to 6
- coarse_inverse: float32 [512, 512], P('coarse'), may hold values from -0.25 to 0.25
- partner: int32 [8, 4], P('sub'), may hold values from 0 to 7, as said below
- margin_width: int32 [8, 4], P('sub'), may hold values from 4 to 8, as said below
- margin_blocks: int32 [8, 4, 4, 8], P('sub', 'coarse'), may hold values from 0 to 127
- aggregate: int32 [8, 4, 128], P('sub', 'coarse'), may hold values from 0 to 511, as said below
Outputs:
- solution: float32 [8, 4, 128, 128], P('sub', 'coarse')
Inputs may be any that keep to these rules, and one draw needn't show every extreme that they name: partner[s, r] differs from s, partner[partner[s, r], r] = s, and the 4 partners of one subdomain are distinct. margin_width[partner[s, r], r] = margin_width[s, r]; every colour round has a pair with width 8. `margin_blocks`: entries with w >= margin_width[s, r] are not used. aggregate[s, c, b] lies in (s * 4 + c) * 16 to (s * 4 + c + 1) * 16 - 1, and every one of these 16 aggregates has a block of part [s, c].
All inputs are finite; a program needn't handle non-finite values.
Results may differ from a plain program's by a relative error of at most 0.0003.
Values sent between devices are 32-bit elements; how exact they have to be, the bound alone decides.
No kernel may reach another device: no remote copies, remote signals or barrier semaphores. Data moves between devices by JAX's collectives and lax.ppermute only.
A program may use at most 64 MiB of HBM per device.

v0:
```python
import jax
import jax.numpy as jnp
from jax import lax
from jax.sharding import PartitionSpec as P

BS = 128
BPD = 128
AGG_DEV = 16
ITERS = 4


def givens_solve(columns, beta):
    steps_count = len(columns)
    cosines = []
    sines = []
    side_terms = [beta] + [jnp.zeros_like(beta) for unused in range(steps_count)]
    triangle = []
    for column_id in range(steps_count):
        column = list(columns[column_id])
        for row_id in range(column_id):
            upper = column[row_id]
            lower = column[row_id + 1]
            column[row_id] = cosines[row_id] * upper + sines[row_id] * lower
            column[row_id + 1] = cosines[row_id] * lower - sines[row_id] * upper
        upper = column[column_id]
        lower = column[column_id + 1]
        radius = jnp.sqrt(upper * upper + lower * lower)
        cosine = upper / radius
        sine_value = lower / radius
        column[column_id] = radius
        cosines.append(cosine)
        sines.append(sine_value)
        side_terms[column_id + 1] = -sine_value * side_terms[column_id]
        side_terms[column_id] = cosine * side_terms[column_id]
        triangle.append(column)
    weights = [None] * steps_count
    for column_id in reversed(range(steps_count)):
        running = side_terms[column_id]
        for later_col in range(column_id + 1, steps_count):
            running = running - triangle[later_col][column_id] * weights[later_col]
        weights[column_id] = running / triangle[column_id][column_id]
    return weights


def on_device(
    right_side,
    diagonal,
    cell_link,
    block_inverse,
    coupling,
    coarse_basis,
    coarse_inverse,
    partner,
    margin_width,
    margin_blocks,
    aggregate,
):
    highest = lax.Precision.HIGHEST
    block_count = right_side.shape[2]
    unknowns = right_side.shape[3]
    factor = (BS * BPD / AGG_DEV) ** (-0.5)
    inverse_blocks = block_inverse[0, 0]
    couplings = coupling[0, 0]
    basis_local = coarse_basis[0, 0]
    diagonal_local = diagonal[0, 0]
    link_local = cell_link[0, 0]
    paired = partner[0]
    widths = margin_width[0]
    blocks = margin_blocks[0, 0]
    member_of = aggregate[0, 0]
    aggregate_count = coarse_inverse.shape[1]
    member_table = (member_of[:, None] == jnp.arange(aggregate_count)[None, :]).astype(jnp.float32)
    rounds = blocks.shape[0]
    widest = blocks.shape[1]
    target = (blocks.reshape(-1)[:, None] == jnp.arange(block_count)[None, :]).astype(jnp.float32)
    live_mask = (jnp.arange(widest)[None, :] < widths[:, None]).astype(jnp.float32)

    def margin(values):
        outgoing = jnp.take(values, blocks.reshape(-1), axis=0).reshape(rounds, widest, unknowns)
        pieces = []
        for round_id in range(rounds):
            gathered = lax.all_gather(outgoing[round_id], "sub", axis=0, tiled=True)
            pieces.append(lax.dynamic_slice_in_dim(gathered, paired[round_id] * widest, widest, 0))
        incoming = jnp.stack(pieces)
        mapped = (
            jnp.einsum("rij,rwj->rwi", couplings, incoming, precision=highest)
            * live_mask[:, :, None]
        )
        return jnp.einsum(
            "kb,ki->bi", target, mapped.reshape(rounds * widest, unknowns), precision=highest
        )

    def squared_norm(values):
        return lax.psum(jnp.sum(values * values), ("sub", "coarse"))

    start_vector = right_side[0, 0]
    directions = []
    columns = []
    beta = jnp.sqrt(squared_norm(start_vector))
    basis_list = [start_vector / beta]
    for krylov_step in range(ITERS):
        current = basis_list[-1]
        inner = jnp.sum(basis_local * current, axis=1)
        restricted = lax.psum(
            jnp.dot(inner, member_table, precision=highest) * factor, ("sub", "coarse")
        )
        local_part = jnp.einsum(
            "bij,bj->bi", inverse_blocks, current + margin(current), precision=highest
        )
        coarse_part = jnp.dot(coarse_inverse, restricted, precision=highest)
        coarse_full = lax.all_gather(coarse_part, "coarse", axis=0, tiled=True)
        prolonged = jnp.dot(member_table, coarse_full, precision=highest)
        direction = local_part + prolonged[:, None] * basis_local
        directions.append(direction)
        flat_line = direction.reshape(-1)
        link_line = link_local.reshape(-1)
        zero_pad = jnp.zeros((1,), jnp.float32)
        ahead_terms = jnp.concatenate([flat_line[1:], zero_pad]) * link_line
        behind_terms = jnp.concatenate([zero_pad, (link_line * flat_line)[:-1]])
        product = (
            diagonal_local * direction
            - (ahead_terms + behind_terms).reshape(direction.shape)
            - margin(direction)
        )
        projected = lax.psum(
            jnp.stack([jnp.sum(vector * product) for vector in basis_list]), ("sub", "coarse")
        )
        for position in range(len(basis_list)):
            product = product - projected[position] * basis_list[position]
        norm_new = jnp.sqrt(squared_norm(product))
        columns.append([projected[position] for position in range(len(basis_list))] + [norm_new])
        basis_list.append(product / norm_new)
    weights = givens_solve(columns, beta)
    solution = weights[0] * directions[0]
    for position in range(1, ITERS):
        solution = solution + weights[position] * directions[position]
    return solution.reshape(right_side.shape)


def solution(mesh):
    placed = (
        P("sub", "coarse", None, None),
        P("sub", "coarse", None, None),
        P("sub", "coarse", None, None),
        P("sub", "coarse", None, None, None),
        P("sub", "coarse", None, None, None),
        P("sub", "coarse", None, None),
        P("coarse", None),
        P("sub", None),
        P("sub", None),
        P("sub", "coarse", None, None),
        P("sub", "coarse", None),
    )
    return jax.shard_map(
        on_device,
        mesh=mesh,
        in_specs=placed,
        out_specs=P("sub", "coarse", None, None),
        check_vma=False,
    )
```

profile of v0, /device:TPU:0, one launch (start us, length us, event | category | flops | bytes accessed | tf_op | source)
XLA Modules:
  0.0 958.9 jit_solution(15861982066872133460)
XLA Ops:
  0.9 1.5 multiply_reduce_fusion.14
  2.3 42.2 %psum.91 = f32[]{:T(128)} all-reduce(f32[]{:T(128)} %multiply_reduce_fusion.14), channel_id=1, replica_groups=mesh['sub'=8,'coarse'=4] {'sub','coarse'}, use_global_device_ids=true, to_apply=%region_1.0 | all-reduce | flops 1 | bytes 8 | tf_op jit(solution)/shard_map/psum | solution.py:94
  46.9 10.0 %all_gather.108 = f32[64,128]{1,0:T(8,128)S(1)} all-gather(f32[8,128]{1,0:T(8,128)S(1)} %get-tuple-element.63), channel_id=1, replica_groups=mesh['sub'=8,'coarse'=4] {'sub'}, dimensions={0}, use_global_device_ids=true | all-gather | bytes 36864 | tf_op jit(solution)/shard_map/all_gather | solution.py:82
  56.9 1.5 fusion.188
  59.0 8.1 all_gather.109
  67.9 9.1 all_gather.110
  77.6 8.1 all_gather.111
  87.8 15.4 %fusion.6 = f32[128,1,128]{2,1,0:T(1,128)S(1)} fusion(f32[128,128,1]{1,2,0:T(1,128)S(1)} %bitcast.355, f32[1,1,128,128,128]{4,3,2,1,0:T(8,128)} %param.16), kind=kOutput, calls=%fused_computation.14 | convolution fusion | flops 25165824 | bytes 8519680 | tf_op jit(solution)/shard_map/bij,bj->bi/dot_general | solution.py:107
  103.5 39.4 %psum.92 = f32[512]{0:T(512)S(1)} all-reduce(f32[512]{0:T(512)S(1)} %broadcast_multiply_fusion.3), channel_id=1, replica_groups=mesh['sub'=8,'coarse'=4] {'sub','coarse'}, use_global_device_ids=true, to_apply=%region_3.5 | all-reduce | flops 512 | bytes 4096 | tf_op jit(solution)/shard_map/psum | solution.py:104
  143.1 9.8 %all-gather = f32[4,1,128]{2,1,0:T(1,128)S(1)} all-gather(f32[1,1,128]{2,1,0:T(1,128)S(1)} %convolution_bitcast_fusion.7), channel_id=1, replica_groups=mesh['sub'=8,'coarse'=4] {'coarse'}, dimensions={0}, use_global_device_ids=true | all-gather | bytes 2560 | tf_op jit(solution)/shard_map/all_gather | solution.py:111
  153.9 9.8 %all_gather.113 = f32[64,128]{1,0:T(8,128)S(1)} all-gather(f32[8,128]{1,0:T(8,128)S(1)} %get-tuple-element.59), channel_id=1, replica_groups=mesh['sub'=8,'coarse'=4] {'sub'}, dimensions={0}, use_global_device_ids=true | all-gather | bytes 36864 | tf_op jit(solution)/shard_map/all_gather | solution.py:82
  163.8 9.1 all_gather.114
  172.8 8.1 all_gather.115
  180.9 9.1 all_gather.116
  191.5 37.8 %psum.93 = f32[]{:T(128)} all-reduce(f32[]{:T(128)} %get-tuple-element.80), channel_id=1, replica_groups=mesh['sub'=8,'coarse'=4] {'sub','coarse'}, use_global_device_ids=true, to_apply=%region_5.7 | all-reduce | flops 1 | bytes 8 | tf_op jit(solution)/shard_map/psum | solution.py:125
  229.3 1.3 multiply_reduce_fusion.12
  230.6 41.2 %psum.94 = f32[]{:T(128)} all-reduce(f32[]{:T(128)} %multiply_reduce_fusion.12), channel_id=1, replica_groups=mesh['sub'=8,'coarse'=4] {'sub','coarse'}, use_global_device_ids=true, to_apply=%region_7.9 | all-reduce | flops 1 | bytes 8 | tf_op jit(solution)/shard_map/psum | solution.py:94
  274.0 10.1 %all_gather.117 = f32[64,128]{1,0:T(8,128)S(1)} all-gather(f32[8,128]{1,0:T(8,128)S(1)} %get-tuple-element.55), channel_id=1, replica_groups=mesh['sub'=8,'coarse'=4] {'sub'}, dimensions={0}, use_global_device_ids=true | all-gather | bytes 36864 | tf_op jit(solution)/shard_map/all_gather | solution.py:82
  284.1 9.0 all_gather.118
  293.1 8.1 all_gather.119
  301.2 9.0 all_gather.120
  311.1 15.4 %fusion.4 = f32[128,1,128]{2,1,0:T(1,128)S(1)} fusion(f32[128,128,1]{1,2,0:T(1,128)S(1)} %bitcast.356, f32[1,1,128,128,128]{4,3,2,1,0:T(8,128)} %param.16), kind=kOutput, calls=%fused_computation.12 | convolution fusion | flops 25165824 | bytes 8519680 | tf_op jit(solution)/shard_map/bij,bj->bi/dot_general | solution.py:107
  326.8 37.7 %psum.95 = f32[512]{0:T(512)S(1)} all-reduce(f32[512]{0:T(512)S(1)} %broadcast_multiply_fusion.2), channel_id=1, replica_groups=mesh['sub'=8,'coarse'=4] {'sub','coarse'}, use_global_device_ids=true, to_apply=%region_9.11 | all-reduce | flops 512 | bytes 4096 | tf_op jit(solution)/shard_map/psum | solution.py:104
  364.7 9.6 %all-gather.1 = f32[4,1,128]{2,1,0:T(1,128)S(1)} all-gather(f32[1,1,128]{2,1,0:T(1,128)S(1)} %convolution_bitcast_fusion.5), channel_id=1, replica_groups=mesh['sub'=8,'coarse'=4] {'coarse'}, dimensions={0}, use_global_device_ids=true | all-gather | bytes 2560 | tf_op jit(solution)/shard_map/all_gather | solution.py:111
  375.4 9.8 %all_gather.122 = f32[64,128]{1,0:T(8,128)S(1)} all-gather(f32[8,128]{1,0:T(8,128)S(1)} %get-tuple-element.51), channel_id=1, replica_groups=mesh['sub'=8,'coarse'=4] {'sub'}, dimensions={0}, use_global_device_ids=true | all-gather | bytes 36864 | tf_op jit(solution)/shard_map/all_gather | solution.py:82
  385.2 8.1 all_gather.123
  393.3 9.0 all_gather.124
  402.3 8.3 all_gather.125
  411.2 1.0 multiply_reduce_fusion.11
  412.2 1.3 pad_maximum_fusion.8
  413.5 37.6 %psum.96 = f32[2]{0:T(128)S(1)} all-reduce(f32[2]{0:T(128)S(1)} %pad_maximum_fusion.8), channel_id=1, replica_groups=mesh['sub'=8,'coarse'=4] {'sub','coarse'}, use_global_device_ids=true, to_apply=%region_12.14 | all-reduce | flops 2 | bytes 16 | tf_op jit(solution)/shard_map/psum | solution.py:125
  451.8 1.9 multiply_reduce_fusion.9
  453.6 41.7 %psum.97 = f32[]{:T(128)} all-reduce(f32[]{:T(128)} %get-tuple-element.21), channel_id=1, replica_groups=mesh['sub'=8,'coarse'=4] {'sub','coarse'}, use_global_device_ids=true, to_apply=%region_14.16 | all-reduce | flops 1 | bytes 8 | tf_op jit(solution)/shard_map/psum | solution.py:94
  496.8 10.1 %all_gather.126 = f32[64,128]{1,0:T(8,128)S(1)} all-gather(f32[8,128]{1,0:T(8,128)S(1)} %get-tuple-element.47), channel_id=1, replica_groups=mesh['sub'=8,'coarse'=4] {'sub'}, dimensions={0}, use_global_device_ids=true | all-gather | bytes 36864 | tf_op jit(solution)/shard_map/all_gather | solution.py:82
  506.9 8.1 all_gather.127
  515.0 9.0 all_gather.128
  524.0 8.1 all_gather.129
  533.0 15.4 %fusion.2 = f32[128,1,128]{2,1,0:T(1,128)S(1)} fusion(f32[128,128,1]{1,2,0:T(1,128)S(1)} %bitcast.357, f32[1,1,128,128,128]{4,3,2,1,0:T(8,128)} %param.16), kind=kOutput, calls=%fused_computation.10 | convolution fusion | flops 25165824 | bytes 8519680 | tf_op jit(solution)/shard_map/bij,bj->bi/dot_general | solution.py:107
  548.6 37.7 %psum.98 = f32[512]{0:T(512)S(1)} all-reduce(f32[512]{0:T(512)S(1)} %broadcast_multiply_fusion.1), channel_id=1, replica_groups=mesh['sub'=8,'coarse'=4] {'sub','coarse'}, use_global_device_ids=true, to_apply=%region_16.18 | all-reduce | flops 512 | bytes 4096 | tf_op jit(solution)/shard_map/psum | solution.py:104
  586.5 9.6 %all-gather.2 = f32[4,1,128]{2,1,0:T(1,128)S(1)} all-gather(f32[1,1,128]{2,1,0:T(1,128)S(1)} %convolution_bitcast_fusion.3), channel_id=1, replica_groups=mesh['sub'=8,'coarse'=4] {'coarse'}, dimensions={0}, use_global_device_ids=true | all-gather | bytes 2560 | tf_op jit(solution)/shard_map/all_gather | solution.py:111
  597.2 9.8 %all_gather.131 = f32[64,128]{1,0:T(8,128)S(1)} all-gather(f32[8,128]{1,0:T(8,128)S(1)} %get-tuple-element.43), channel_id=1, replica_groups=mesh['sub'=8,'coarse'=4] {'sub'}, dimensions={0}, use_global_device_ids=true | all-gather | bytes 36864 | tf_op jit(solution)/shard_map/all_gather | solution.py:82
  607.0 9.0 all_gather.132
  616.1 8.5 all_gather.133
  624.6 9.0 all_gather.134
  635.2 1.9 pad_maximum_fusion.9
  637.2 37.6 %psum.99 = f32[3]{0:T(128)S(1)} all-reduce(f32[3]{0:T(128)S(1)} %pad_maximum_fusion.9), channel_id=1, replica_groups=mesh['sub'=8,'coarse'=4] {'sub','coarse'}, use_global_device_ids=true, to_apply=%region_20.22 | all-reduce | flops 3 | bytes 24 | tf_op jit(solution)/shard_map/psum | solution.py:125
  675.4 2.5 multiply_reduce_fusion.5
  677.9 40.7 %psum.100 = f32[]{:T(128)} all-reduce(f32[]{:T(128)} %get-tuple-element.17), channel_id=1, replica_groups=mesh['sub'=8,'coarse'=4] {'sub','coarse'}, use_global_device_ids=true, to_apply=%region_22.24 | all-reduce | flops 1 | bytes 8 | tf_op jit(solution)/shard_map/psum | solution.py:94
  720.0 10.0 %all_gather.135 = f32[64,128]{1,0:T(8,128)S(1)} all-gather(f32[8,128]{1,0:T(8,128)S(1)} %get-tuple-element.39), channel_id=1, replica_groups=mesh['sub'=8,'coarse'=4] {'sub'}, dimensions={0}, use_global_device_ids=true | all-gather | bytes 36864 | tf_op jit(solution)/shard_map/all_gather | solution.py:82
  730.0 9.0 all_gather.136
  739.1 8.1 all_gather.137
  747.1 9.0 all_gather.138
  757.1 15.4 %fusion = f32[128,1,128]{2,1,0:T(1,128)S(1)} fusion(f32[128,128,1]{1,2,0:T(1,128)S(1)} %bitcast.358, f32[1,1,128,128,128]{4,3,2,1,0:T(8,128)} %param.16), kind=kOutput, calls=%fused_computation.8 | convolution fusion | flops 25165824 | bytes 8519680 | tf_op jit(solution)/shard_map/bij,bj->bi/dot_general | solution.py:107
  772.7 37.7 %psum.101 = f32[512]{0:T(512)S(1)} all-reduce(f32[512]{0:T(512)S(1)} %broadcast_multiply_fusion), channel_id=1, replica_groups=mesh['sub'=8,'coarse'=4] {'sub','coarse'}, use_global_device_ids=true, to_apply=%region_24.26 | all-reduce | flops 512 | bytes 4096 | tf_op jit(solution)/shard_map/psum | solution.py:104
  810.6 9.6 %all-gather.3 = f32[4,1,128]{2,1,0:T(1,128)S(1)} all-gather(f32[1,1,128]{2,1,0:T(1,128)S(1)} %convolution_bitcast_fusion.1), channel_id=1, replica_groups=mesh['sub'=8,'coarse'=4] {'coarse'}, dimensions={0}, use_global_device_ids=true | all-gather | bytes 2560 | tf_op jit(solution)/shard_map/all_gather | solution.py:111
  821.3 9.8 %all_gather.140 = f32[64,128]{1,0:T(8,128)S(1)} all-gather(f32[8,128]{1,0:T(8,128)S(1)} %get-tuple-element.35), channel_id=1, replica_groups=mesh['sub'=8,'coarse'=4] {'sub'}, dimensions={0}, use_global_device_ids=true | all-gather | bytes 36864 | tf_op jit(solution)/shard_map/all_gather | solution.py:82
  831.1 8.2 all_gather.141
  839.4 9.0 all_gather.142
  848.4 8.1 all_gather.143
  857.1 1.0 multiply_reduce_fusion.4
  858.1 2.5 pad_maximum_fusion.10
  860.6 37.6 %psum.102 = f32[4]{0:T(128)S(1)} all-reduce(f32[4]{0:T(128)S(1)} %pad_maximum_fusion.10), channel_id=1, replica_groups=mesh['sub'=8,'coarse'=4] {'sub','coarse'}, use_global_device_ids=true, to_apply=%region_29.31 | all-reduce | flops 4 | bytes 32 | tf_op jit(solution)/shard_map/psum | solution.py:125
  905.5 3.0 multiply_reduce_fusion
  908.5 41.8 %psum.103 = f32[]{:T(128)} all-reduce(f32[]{:T(128)} %multiply_reduce_fusion), channel_id=1, replica_groups=mesh['sub'=8,'coarse'=4] {'sub','coarse'}, use_global_device_ids=true, to_apply=%region_31.33 | all-reduce | flops 1 | bytes 8 | tf_op jit(solution)/shard_map/psum | solution.py:94
  (119 shorter events, 22.8 us)
Async XLA Ops:
  0.0 87.0 %copy-start = (f32[1,1,4,128,128]{4,3,2,1,0:T(8,128)S(1)}, f32[1,1,4,128,128]{4,3,2,1,0:T(8,128)}, u32[]{:S(2)}) copy-start(f32[1,1,4,128,128]{4,3,2,1,0:T(8,128)} %param.17) | copy-start | bytes 786436
  0.0 153.1 %copy-start.1 = (f32[1,1,128,128]{3,2,1,0:T(8,128)S(1)}, f32[1,1,128,128]{3,2,1,0:T(8,128)}, u32[]{:S(2)}) copy-start(f32[1,1,128,128]{3,2,1,0:T(8,128)} %param.18) | copy-start | bytes 196612
  0.0 103.2 %copy-start.5 = (s32[1,1,128]{2,1,0:T(1,128)S(1)}, s32[1,1,128]{2,1,0:T(1,128)}, u32[]{:S(2)}) copy-start(s32[1,1,128]{2,1,0:T(1,128)} %param.23) | copy-start | bytes 1540
  0.0 142.9 %copy-start.2 = (f32[128,512]{1,0:T(8,128)S(1)}, f32[128,512]{1,0:T(8,128)}, u32[]{:S(2)}) copy-start(f32[128,512]{1,0:T(8,128)} %param.19) | copy-start | bytes 786436
  0.0 190.4 %copy-start.3 = (f32[1,1,128,128]{3,2,1,0:T(8,128)S(1)}, f32[1,1,128,128]{3,2,1,0:T(8,128)}, u32[]{:S(2)}) copy-start(f32[1,1,128,128]{3,2,1,0:T(8,128)} %param.15) | copy-start | bytes 196612
  0.0 190.5 %copy-start.4 = (f32[1,1,128,128]{3,2,1,0:T(8,128)S(1)}, f32[1,1,128,128]{3,2,1,0:T(8,128)}, u32[]{:S(2)}) copy-start(f32[1,1,128,128]{3,2,1,0:T(8,128)} %param.14) | copy-start | bytes 196612
where the time goes:
time: 971 us; the launch traced here: 959 us
  blocking collectives  835 us (86%)
  matrix products  73.9 us (8%)
  other arithmetic  21.1 us (2%)
  between operations  20.1 us (2%)
    all_gather x32, blocking collectives, margin(): gathered = lax.all_gather(outgoing[round_id], 'sub', axis=0, tiled=True)  286 us
    psum x5, blocking collectives, squared_norm(): return lax.psum(jnp.sum(values * values), ('sub', 'coarse'))  208 us
    psum x4, blocking collectives, on_device(): lax.psum(jnp.dot(inner, member_table, precision=highest) * factor, ('sub'...  152 us
    psum x4, blocking collectives, on_device(): lax.psum(jnp.stack([jnp.sum(vector * product) for vector in basis_list]),...  151 us
    dot_general x4, matrix products, on_device(): jnp.einsum('bij,bj->bi', inverse_blocks, current + margin(current), preci...  61.5 us
    all_gather x4, blocking collectives, on_device(): coarse_full = lax.all_gather(coarse_part, 'coarse', axis=0, tiled=True)  38.7 us

commit v1 on v0

--- a/solution.py
+++ b/solution.py
@@ -108,7 +108,21 @@
             "bij,bj->bi", inverse_blocks, current + margin(current), precision=highest
         )
         coarse_part = jnp.dot(coarse_inverse, restricted, precision=highest)
-        coarse_full = lax.all_gather(coarse_part, "coarse", axis=0, tiled=True)
+        all_values = lax.axis_size("coarse")
+        v_now = lax.axis_index("coarse")
+        taken_in, g_now, z1 = (all_values, v_now, coarse_part.shape[0])
+        tray = tuple(((jj, (jj + 1) % taken_in) for jj in range(taken_in)))
+        coarse_full = jnp.zeros(
+            (*coarse_part.shape[:0], taken_in * z1, *coarse_part.shape[0 + 1 :]), coarse_part.dtype
+        )
+        found_now = coarse_part
+        for pp in [*range(taken_in)]:
+            local_next = (g_now - pp) % taken_in
+            coarse_full = lax.dynamic_update_slice_in_dim(
+                coarse_full, found_now, local_next * z1, axis=0
+            )
+            if pp < taken_in - 1:
+                found_now = lax.ppermute(found_now, "coarse", tray)
         prolonged = jnp.dot(member_table, coarse_full, precision=highest)
         direction = local_part + prolonged[:, None] * basis_local
         directions.append(direction)

time: 971 us -> 938 us (0.966)
  matrix products: 73.9 us -> 13.6 us
  blocking collectives: 835 us -> 796 us
  waiting for transfers between devices: 0 us -> 25.1 us
  other arithmetic: 21.1 us -> 42.4 us
  starting transfers between devices: 0 us -> 10.6 us
    dot_general x4 -> x0, matrix products: 61.5 us -> none  [on_device(): jnp.einsum('bij,bj->bi', inverse_blocks, current + margin(current), preci...]
    all_gather x4 -> x0, blocking collectives: 38.7 us -> none  [on_device(): coarse_full = lax.all_gather(coarse_part, 'coarse', axis=0, tiled=True)]
    ppermute x0 -> x12, waiting for transfers between devices: none -> 25.1 us  [on_device(): found_now = lax.ppermute(found_now, 'coarse', tray)]
    unnamed x0 -> x4, other arithmetic: none -> 22.5 us
    ppermute x0 -> x12, starting transfers between devices: none -> 10.6 us  [on_device(): found_now = lax.ppermute(found_now, 'coarse', tray)]
  transfers between devices with their start and end apart: 0 -> 12, of which waited for: 0 -> 6; matrix products, arithmetic and copies ran while one was open for 0% -> 4% of each run, Pallas kernels for 0% -> 0%
where the time goes in v1:
time: 938 us; the launch traced here: 926 us
  blocking collectives  796 us (85%)
  other arithmetic  42.4 us (5%)
  waiting for transfers between devices  25.1 us (3%)
  between operations  21.1 us (2%)
  local copies, waits for them, and re-layouts  17.3 us (2%)
  matrix products  13.6 us (1%)
  starting transfers between devices  10.6 us (1%)
    all_gather x32, blocking collectives, margin(): gathered = lax.all_gather(outgoing[round_id], 'sub', axis=0, tiled=True)  279 us
    psum x5, blocking collectives, squared_norm(): return lax.psum(jnp.sum(values * values), ('sub', 'coarse'))  211 us
    psum x4, blocking collectives, on_device(): lax.psum(jnp.dot(inner, member_table, precision=highest) * factor, ('sub'...  158 us
    psum x4, blocking collectives, on_device(): lax.psum(jnp.stack([jnp.sum(vector * product) for vector in basis_list]),...  148 us
    ppermute x12, waiting for transfers between devices, on_device(): found_now = lax.ppermute(found_now, 'coarse', tray)  25.1 us
    unnamed x4, other arithmetic  22.5 us
  transfers between devices with their start and end apart: 12, of which 6 were waited for; matrix products, arithmetic and copies ran while one was open for 4% of the time, Pallas kernels for 0%

profile of v1, /device:TPU:0, one launch (start us, length us, event | category | flops | bytes accessed | tf_op | source)
XLA Modules:
  0.0 926.2 jit_solution(8619355242627927982)
XLA Ops:
  0.0 1.5 multiply_reduce_fusion.14
  2.5 42.3 %psum.91 = f32[]{:T(128)} all-reduce(f32[]{:T(128)} %multiply_reduce_fusion.14), channel_id=1, replica_groups=mesh['sub'=8,'coarse'=4] {'sub','coarse'}, use_global_device_ids=true, to_apply=%region_1.0 | all-reduce | flops 1 | bytes 8 | tf_op jit(solution)/shard_map/psum | solution.py:94
  47.3 40.3 %psum.92 = f32[512]{0:T(512)S(1)} all-reduce(f32[512]{0:T(512)S(1)} %broadcast_multiply_fusion.3), channel_id=1, replica_groups=mesh['sub'=8,'coarse'=4] {'sub','coarse'}, use_global_device_ids=true, to_apply=%region_3.5 | all-reduce | flops 512 | bytes 4096 | tf_op jit(solution)/shard_map/psum | solution.py:104
  95.8 9.8 %all_gather.96 = f32[64,128]{1,0:T(8,128)S(1)} all-gather(f32[8,128]{1,0:T(8,128)S(1)} %get-tuple-element.63), channel_id=1, replica_groups=mesh['sub'=8,'coarse'=4] {'sub'}, dimensions={0}, use_global_device_ids=true | all-gather | bytes 36864 | tf_op jit(solution)/shard_map/all_gather | solution.py:82
  105.6 9.0 all_gather.99
  114.6 8.1 all_gather.98
  122.7 9.0 all_gather.97
  132.6 5.6 fusion
  139.8 3.9 collective-permute-done.1
  144.4 4.6 collective-permute-done.2
  150.3 8.1 all_gather.100
  158.4 9.0 all_gather.103
  167.4 8.1 all_gather.102
  175.5 9.0 all_gather.101
  186.3 37.1 %psum.93 = f32[]{:T(128)} all-reduce(f32[]{:T(128)} %get-tuple-element.80), channel_id=1, replica_groups=mesh['sub'=8,'coarse'=4] {'sub','coarse'}, use_global_device_ids=true, to_apply=%region_5.7 | all-reduce | flops 1 | bytes 8 | tf_op jit(solution)/shard_map/psum | solution.py:139
  224.7 42.3 %psum.94 = f32[]{:T(128)} all-reduce(f32[]{:T(128)} %multiply_reduce_fusion.12), channel_id=1, replica_groups=mesh['sub'=8,'coarse'=4] {'sub','coarse'}, use_global_device_ids=true, to_apply=%region_7.9 | all-reduce | flops 1 | bytes 8 | tf_op jit(solution)/shard_map/psum | solution.py:94
  268.7 39.6 %psum.95 = f32[512]{0:T(512)S(1)} all-reduce(f32[512]{0:T(512)S(1)} %broadcast_multiply_fusion.2), channel_id=1, replica_groups=mesh['sub'=8,'coarse'=4] {'sub','coarse'}, use_global_device_ids=true, to_apply=%region_9.11 | all-reduce | flops 512 | bytes 4096 | tf_op jit(solution)/shard_map/psum | solution.py:104
  308.5 2.2 collective-permute-start.3
  311.4 9.8 %all_gather.104 = f32[64,128]{1,0:T(8,128)S(1)} all-gather(f32[8,128]{1,0:T(8,128)S(1)} %get-tuple-element.55), channel_id=1, replica_groups=mesh['sub'=8,'coarse'=4] {'sub'}, dimensions={0}, use_global_device_ids=true | all-gather | bytes 36864 | tf_op jit(solution)/shard_map/all_gather | solution.py:82
  321.3 8.1 all_gather.107
  329.4 9.0 all_gather.106
  338.4 8.1 all_gather.105
  348.1 5.6 fusion.1
  356.7 3.8 collective-permute-done.5
  361.7 9.0 all_gather.108
  370.7 8.1 all_gather.111
  378.8 9.0 all_gather.110
  387.8 8.1 all_gather.109
  399.3 36.8 %psum.96 = f32[2]{0:T(128)S(1)} all-reduce(f32[2]{0:T(128)S(1)} %pad_maximum_fusion.8), channel_id=1, replica_groups=mesh['sub'=8,'coarse'=4] {'sub','coarse'}, use_global_device_ids=true, to_apply=%region_12.14 | all-reduce | flops 2 | bytes 16 | tf_op jit(solution)/shard_map/psum | solution.py:139
  436.8 1.9 multiply_reduce_fusion.9
  438.8 42.4 %psum.97 = f32[]{:T(128)} all-reduce(f32[]{:T(128)} %get-tuple-element.21), channel_id=1, replica_groups=mesh['sub'=8,'coarse'=4] {'sub','coarse'}, use_global_device_ids=true, to_apply=%region_14.16 | all-reduce | flops 1 | bytes 8 | tf_op jit(solution)/shard_map/psum | solution.py:94
  482.1 38.9 %psum.98 = f32[512]{0:T(512)S(1)} all-reduce(f32[512]{0:T(512)S(1)} %broadcast_multiply_fusion.1), channel_id=1, replica_groups=mesh['sub'=8,'coarse'=4] {'sub','coarse'}, use_global_device_ids=true, to_apply=%region_16.18 | all-reduce | flops 512 | bytes 4096 | tf_op jit(solution)/shard_map/psum | solution.py:104
  521.3 2.2 collective-permute-start.6
  524.2 9.8 %all_gather.112 = f32[64,128]{1,0:T(8,128)S(1)} all-gather(f32[8,128]{1,0:T(8,128)S(1)} %get-tuple-element.47), channel_id=1, replica_groups=mesh['sub'=8,'coarse'=4] {'sub'}, dimensions={0}, use_global_device_ids=true | all-gather | bytes 36864 | tf_op jit(solution)/shard_map/all_gather | solution.py:82
  534.0 9.0 all_gather.115
  543.0 8.1 all_gather.114
  551.1 9.0 all_gather.113
  561.7 5.6 fusion.2
  571.0 4.4 collective-permute-done.8
  576.7 8.1 all_gather.116
  584.9 9.0 all_gather.119
  593.8 8.1 all_gather.118
  602.0 9.0 all_gather.117
  612.9 2.0 pad_maximum_fusion.9
  614.9 36.8 %psum.99 = f32[3]{0:T(128)S(1)} all-reduce(f32[3]{0:T(128)S(1)} %pad_maximum_fusion.9), channel_id=1, replica_groups=mesh['sub'=8,'coarse'=4] {'sub','coarse'}, use_global_device_ids=true, to_apply=%region_20.22 | all-reduce | flops 3 | bytes 24 | tf_op jit(solution)/shard_map/psum | solution.py:139
  652.4 2.5 multiply_reduce_fusion.5
  654.9 41.6 %psum.100 = f32[]{:T(128)} all-reduce(f32[]{:T(128)} %get-tuple-element.17), channel_id=1, replica_groups=mesh['sub'=8,'coarse'=4] {'sub','coarse'}, use_global_device_ids=true, to_apply=%region_22.24 | all-reduce | flops 1 | bytes 8 | tf_op jit(solution)/shard_map/psum | solution.py:94
  697.5 39.6 %psum.101 = f32[512]{0:T(512)S(1)} all-reduce(f32[512]{0:T(512)S(1)} %broadcast_multiply_fusion), channel_id=1, replica_groups=mesh['sub'=8,'coarse'=4] {'sub','coarse'}, use_global_device_ids=true, to_apply=%region_24.26 | all-reduce | flops 512 | bytes 4096 | tf_op jit(solution)/shard_map/psum | solution.py:104
  737.3 2.2 collective-permute-start.9
  740.2 10.0 %all_gather.120 = f32[64,128]{1,0:T(8,128)S(1)} all-gather(f32[8,128]{1,0:T(8,128)S(1)} %get-tuple-element.39), channel_id=1, replica_groups=mesh['sub'=8,'coarse'=4] {'sub'}, dimensions={0}, use_global_device_ids=true | all-gather | bytes 36864 | tf_op jit(solution)/shard_map/all_gather | solution.py:82
  750.3 8.1 all_gather.123
  758.4 9.0 all_gather.122
  767.4 8.1 all_gather.121
  776.4 5.6 fusion.3
  786.7 3.9 collective-permute-done.10
  791.5 4.5 collective-permute-done.11
  797.2 9.0 all_gather.124
  806.2 8.1 all_gather.127
  814.3 9.0 all_gather.126
  823.3 8.1 all_gather.125
  833.4 2.6 pad_maximum_fusion.10
  836.0 36.8 %psum.102 = f32[4]{0:T(128)S(1)} all-reduce(f32[4]{0:T(128)S(1)} %pad_maximum_fusion.10), channel_id=1, replica_groups=mesh['sub'=8,'coarse'=4] {'sub','coarse'}, use_global_device_ids=true, to_apply=%region_29.31 | all-reduce | flops 4 | bytes 32 | tf_op jit(solution)/shard_map/psum | solution.py:139
  878.6 3.2 multiply_reduce_fusion
  881.8 42.5 %psum.103 = f32[]{:T(128)} all-reduce(f32[]{:T(128)} %multiply_reduce_fusion), channel_id=1, replica_groups=mesh['sub'=8,'coarse'=4] {'sub','coarse'}, use_global_device_ids=true, to_apply=%region_31.33 | all-reduce | flops 1 | bytes 8 | tf_op jit(solution)/shard_map/psum | solution.py:94
  (193 shorter events, 41.2 us)
Async XLA Ops:
  0.0 131.7 %copy-start = (f32[1,1,4,128,128]{4,3,2,1,0:T(8,128)S(1)}, f32[1,1,4,128,128]{4,3,2,1,0:T(8,128)}, u32[]{:S(2)}) copy-start(f32[1,1,4,128,128]{4,3,2,1,0:T(8,128)} %param.17) | copy-start | bytes 786436
  0.0 149.2 %copy-start.4 = (s32[1,1,128]{2,1,0:T(1,128)S(1)}, s32[1,1,128]{2,1,0:T(1,128)}, u32[]{:S(2)}) copy-start(s32[1,1,128]{2,1,0:T(1,128)} %param.23) | copy-start | bytes 1540
  0.0 308.3 %copy-start.1 = (f32[128,512]{1,0:T(8,128)S(1)}, f32[128,512]{1,0:T(8,128)}, u32[]{:S(2)}) copy-start(f32[128,512]{1,0:T(8,128)} %param.19) | copy-start | bytes 786436
  0.0 139.6 %copy-start.3 = (f32[1,1,128,128]{3,2,1,0:T(8,128)S(1)}, f32[1,1,128,128]{3,2,1,0:T(8,128)}, u32[]{:S(2)}) copy-start(f32[1,1,128,128]{3,2,1,0:T(8,128)} %param.14) | copy-start | bytes 196612
  0.0 139.7 %copy-start.2 = (f32[1,1,128,128]{3,2,1,0:T(8,128)S(1)}, f32[1,1,128,128]{3,2,1,0:T(8,128)}, u32[]{:S(2)}) copy-start(f32[1,1,128,128]{3,2,1,0:T(8,128)} %param.15) | copy-start | bytes 196612
  88.9 49.4 %collective-permute-start = (f32[128]{0:T(128)S(1)}, f32[128]{0:T(128)S(1)}, u32[]{:S(2)}, u32[]{:S(2)}) collective-permute-start(f32[128]{0:T(128)S(1)} %convolution_bitcast_fusion.7), channel_id=1, source_target_pairs={{0,1},{1,2},{2,3},{3,0},{4,5},{5,6},{6,7},{7,4},{8,9},{9,10},{10,1... | collective-permute-start | bytes 1544 | tf_op jit(solution)/shard_map/ppermute | solution.py:125
  138.3 5.4 collective-permute-start.1
  143.7 5.3 collective-permute-start.2
  308.5 38.9 %collective-permute-start.3 = (f32[128]{0:T(128)S(1)}, f32[128]{0:T(128)S(1)}, u32[]{:S(2)}, u32[]{:S(2)}) collective-permute-start(f32[128]{0:T(128)S(1)} %convolution_bitcast_fusion.5), channel_id=1, source_target_pairs={{0,1},{1,2},{2,3},{3,0},{4,5},{5,6},{6,7},{7,4},{8,9},{9,10},{10,1... | collective-permute-start | bytes 1544 | tf_op jit(solution)/shard_map/ppermute | solution.py:125
  347.4 7.6 collective-permute-start.4
  355.1 5.4 collective-permute-start.5
  521.3 39.7 %collective-permute-start.6 = (f32[128]{0:T(128)S(1)}, f32[128]{0:T(128)S(1)}, u32[]{:S(2)}, u32[]{:S(2)}) collective-permute-start(f32[128]{0:T(128)S(1)} %convolution_bitcast_fusion.3), channel_id=1, source_target_pairs={{0,1},{1,2},{2,3},{3,0},{4,5},{5,6},{6,7},{7,4},{8,9},{9,10},{10,1... | collective-permute-start | bytes 1544 | tf_op jit(solution)/shard_map/ppermute | solution.py:125
  561.0 9.1 collective-permute-start.7
  570.1 5.4 collective-permute-start.8
  737.3 47.9 %collective-permute-start.9 = (f32[128]{0:T(128)S(1)}, f32[128]{0:T(128)S(1)}, u32[]{:S(2)}, u32[]{:S(2)}) collective-permute-start(f32[128]{0:T(128)S(1)} %convolution_bitcast_fusion.1), channel_id=1, source_target_pairs={{0,1},{1,2},{2,3},{3,0},{4,5},{5,6},{6,7},{7,4},{8,9},{9,10},{10,1... | collective-permute-start | bytes 1544 | tf_op jit(solution)/shard_map/ppermute | solution.py:125
  785.2 5.4 collective-permute-start.10
  790.6 5.3 collective-permute-start.11
